TPU v7x, 32 devices: a whole 2x2x4 slice. The times are simulated.
32 devices in a mesh: dp: 8 (over y, x, core), expert: 4 (over z).
Axes of the slice: x: 2, y: 2, z: 4, core: 2. Of those that a mesh axis runs over, the one named last changes fastest.
Arguments:
- cotangent: bfloat16 [32768, 2048], P(('dp', 'expert')), may hold values from -6 to 6
- route_ids: int32 [32768, 6], P(('dp', 'expert')), may hold values from 0 to 63, all different within a row; in each aligned block of 1024 rows (0 to 1023, 1024 to 2047, ...) at most 192 rows name the same one
- route_weights: float32 [32768, 6], P(('dp', 'expert')), may hold values from 0.02 to 1
- hidden: bfloat16 [8, 6144, 1408], P('expert', 'dp'), may hold values from -6 to 6
- master: float32 [1408, 8, 2048], P('dp', 'expert'), may hold values from -0.3 to 0.3
- first_moment: float32 [1408, 8, 2048], P('dp', 'expert'), may hold values from -1.2 to 1.2
- second_moment: float32 [1408, 8, 2048], P('dp', 'expert'), may hold values from 0.002 to 0.05
Outputs:
- new_master: float32 [1408, 8, 2048], P('dp', 'expert')
- new_first: float32 [1408, 8, 2048], P('dp', 'expert')
- new_second: float32 [1408, 8, 2048], P('dp', 'expert')
Inputs may be any that keep to these rules, and one draw needn't show every extreme that they name: `route_ids`: each row names 6 different experts. Within the 1024 rows of one device no expert is named by more than 192 rows.
All inputs are finite; a program needn't handle non-finite values.
Results may differ from a plain program's by a relative error of at most 0.0019.
Values may be sent and summed in bfloat16 or wider, within the bound.
A program may use at most 128 MiB of HBM per device.

v0:
```python
import jax
import jax.numpy as jnp
from jax import lax
from jax.sharding import PartitionSpec as P

beta_one = 0.9
beta_two = 0.999
learning_rate = 0.001
epsilon = 1e-08
decay_rate = 0.1
step_count = 4.0


def slot_table(route_ids, route_weights, window, capacity, local_count, groups):
    tokens = route_ids.shape[0]
    onehot = (route_ids[:, :, None] == jnp.arange(window, dtype=jnp.int32)[None, None, :]).astype(
        jnp.int32
    )
    counts = jnp.sum(onehot, axis=1)
    before = jnp.cumsum(counts, axis=0) - counts
    ranks = jnp.sum(onehot * before[:, None, :], axis=2)
    inside = route_ids < window
    position = (
        route_ids % local_count * (groups * capacity) + route_ids // local_count * capacity + ranks
    )
    position = jnp.where(inside, position, window * capacity)
    anchor = jnp.broadcast_to(jnp.arange(tokens, dtype=jnp.int32)[:, None], route_ids.shape)
    slot_anchor = (
        jnp.zeros((window * capacity + 1,), jnp.int32)
        .at[position.reshape(-1)]
        .set(anchor.reshape(-1))
    )
    masked = jnp.where(inside, route_weights, jnp.zeros_like(route_weights))
    slot_weight = (
        jnp.zeros((window * capacity + 1,), route_weights.dtype)
        .at[position.reshape(-1)]
        .set(masked.reshape(-1))
    )
    return (slot_anchor[:-1], slot_weight[:-1])


def shards(cotangent, route_ids, route_weights, hidden, master, first_moment, second_moment):
    groups = lax.axis_size("expert")
    local_count = hidden.shape[0]
    capacity = hidden.shape[1] // groups
    width = cotangent.shape[1]
    window = local_count * groups
    owned_rows = master.shape[0]
    slot_anchor, slot_weight = slot_table(
        route_ids, route_weights, window, capacity, local_count, groups
    )
    scaled = (cotangent[slot_anchor].astype(jnp.float32) * slot_weight[:, None]).astype(
        jnp.bfloat16
    )
    scaled = scaled.reshape(local_count, groups * capacity, width)
    received = lax.all_to_all(scaled, "expert", split_axis=1, concat_axis=1, tiled=True)
    pieces = []
    for expert_local in range(local_count):
        hidden_one = hidden[expert_local]
        received_one = received[expert_local]

        def one_term(start, count, hidden_one=hidden_one, received_one=received_one):
            return jnp.einsum(
                "rf,rd->fd", hidden_one, received_one, preferred_element_type=jnp.float32
            )

        pieces.append(
            lax.psum_scatter(
                one_term(jnp.int32(0), owned_rows * lax.axis_size("dp")),
                "dp",
                scatter_dimension=0,
                tiled=True,
            )
        )
    summed = jnp.stack(pieces, axis=1)
    gradient = summed / jnp.sqrt(jnp.float32(groups * capacity))
    new_first = beta_one * first_moment + (1.0 - beta_one) * gradient
    new_second = beta_two * second_moment + (1.0 - beta_two) * gradient * gradient
    corrected_first = new_first / (1.0 - beta_one**step_count)
    corrected_second = new_second / (1.0 - beta_two**step_count)
    update = corrected_first / (jnp.sqrt(corrected_second) + epsilon) + decay_rate * master
    new_master = master - learning_rate * update
    return (new_master, new_first, new_second)


def solution(mesh):
    placed = (
        P(("dp", "expert"), None),
        P(("dp", "expert"), None),
        P(("dp", "expert"), None),
        P("expert", "dp", None),
        P("dp", "expert", None),
        P("dp", "expert", None),
        P("dp", "expert", None),
    )
    return jax.shard_map(
        shards,
        mesh=mesh,
        in_specs=placed,
        out_specs=(P("dp", "expert", None), P("dp", "expert", None), P("dp", "expert", None)),
        check_vma=False,
    )
```

profile of v0, /device:TPU:0, one launch (start us, length us, event | category | flops | bytes accessed | tf_op | source)
XLA Modules:
  0.0 474.1 jit_solution(2417612220993016401)
XLA Ops:
  7.2 0.8 convert_reduce_fusion
  8.0 2.3 reduce-window.6
  10.8 0.8 select_reduce_fusion
  11.7 0.8 fusion.10
  12.5 0.8 broadcast_select_fusion
  13.5 0.3 reshape.92
  14.0 0.4 reshape.68
  14.5 23.0 %scatter_custom_fusion.1 = f32[1537]{0:T(1024)S(1)} fusion(s32[6144]{0:T(1024)S(1)} %bitcast.45, f32[6144]{0:T(1024)S(1)} %reshape.92, f32[]{:T(128)} %constant.62.clone.1), kind=kCustom, calls=%fused_computation.46 | custom fusion | bytes 6152 | tf_op jit(solution)/shard_map/scatter | solution.py:37
  37.8 23.0 %scatter_custom_fusion = s32[1537]{0:T(1024)S(1)} fusion(s32[6144]{0:T(1024)S(1)} %bitcast.46, s32[6144]{0:T(1024)S(1)} %reshape.84, s32[]{:T(128)} %constant.29.clone.1), kind=kCustom, calls=%fused_computation.48 | custom fusion | bytes 6152 | tf_op jit(solution)/shard_map/scatter | solution.py:31
  60.9 15.5 %gather_fusion = bf16[1536,2048]{1,0:T(8,128)(2,1)} fusion(bf16[1024,2048]{1,0:T(8,128)(2,1)} %param.7, s32[2048]{0:T(1024)S(1)} %pad_clamp_fusion), kind=kCustom, calls=%fused_computation | custom fusion | bytes 12589056 | tf_op jit(solution)/shard_map/gather | solution.py:52
  76.3 3.9 fusion
  80.2 13.0 %copy.75 = bf16[2,768,2048]{2,0,1:T(2,128)(2,1)S(1)} copy(bf16[2,768,2048]{2,1,0:T(8,128)(2,1)S(1)} %fusion) | data formatting | bytes 12582912 | tf_op jit(solution)/shard_map/convert_element_type | solution.py:52
  93.3 144.5 %all_to_all.5 = bf16[2,768,2048]{2,0,1:T(2,128)(2,1)S(1)} all-to-all(bf16[2,768,2048]{2,0,1:T(2,128)(2,1)S(1)} %copy.75), channel_id=1, replica_groups=mesh['dp'=8,'expert'=4] {'expert'}, dimensions={1} | all-to-all | bytes 12582912 | tf_op jit(solution)/shard_map/all_to_all | solution.py:56
  237.7 9.7 %fusion.23 = (bf16[1,768,2048]{2,0,1:T(2,128)(2,1)S(1)}, bf16[1,768,2048]{2,0,1:T(2,128)(2,1)}) fusion(bf16[2,768,2048]{2,0,1:T(2,128)(2,1)S(1)} %all_to_all.5), kind=kLoop, calls=%fused_computation.50 | loop fusion | bytes 12582912 | tf_op jit(solution)/shard_map/slice | solution.py:60
  247.5 9.6 %convolution_bitcast_fusion.1 = f32[1408,2048]{0,1:T(8,128)} fusion(bf16[1,768,2048]{2,0,1:T(2,128)(2,1)S(1)} %get-tuple-element.24, bf16[2,768,1408]{2,1,0:T(8,128)(2,1)S(1)} %bitcast.49), kind=kOutput, calls=%fused_computation.6 | convolution fusion | flops 4429185024 | bytes 19988480 | tf_op jit(solution)/shard_map/rf,rd->fd/dot_general | solution.py:63
  257.1 12.0 %copy.86 = f32[1408,2048]{1,0:T(8,128)} copy(f32[1408,2048]{0,1:T(8,128)} %convolution_bitcast_fusion.1) | data formatting | bytes 23068672
  269.2 12.6 %convolution_bitcast_fusion = f32[1408,2048]{0,1:T(8,128)} fusion(bf16[1,768,2048]{2,0,1:T(2,128)(2,1)} %get-tuple-element.25, bf16[2,768,1408]{2,1,0:T(8,128)(2,1)} %param.10), kind=kOutput, calls=%fused_computation.5 | convolution fusion | flops 4429185024 | bytes 19988480 | tf_op jit(solution)/shard_map/rf,rd->fd/dot_general | solution.py:63
  281.8 12.8 %copy.88 = f32[1408,2048]{1,0:T(8,128)} copy(f32[1408,2048]{0,1:T(8,128)} %convolution_bitcast_fusion) | data formatting | bytes 23068672
  294.6 61.4 %reduce-scatter.7.cloned.1.call-done = f32[176,2048]{1,0:T(8,128)} async-done(((f32[1408,2048]{1,0:T(8,128)}), f32[176,2048]{1,0:T(8,128)}) %reduce-scatter.7.cloned.1.call-update) | async-done | bytes 1441808 | tf_op jit(solution)/shard_map/reduce_scatter | solution.py:68
  356.0 90.7 %reduce-scatter.9.cloned.1.call-done = f32[176,2048]{1,0:T(8,128)} async-done(((f32[1408,2048]{1,0:T(8,128)}), f32[176,2048]{1,0:T(8,128)}) %reduce-scatter.9.cloned.1.call-update) | async-done | bytes 1441808 | tf_op jit(solution)/shard_map/reduce_scatter | solution.py:68
  446.7 9.2 %multiply_subtract_fusion = (f32[176,2,2048]{2,0,1:T(8,128)S(1)}, f32[176,2,2048]{2,0,1:T(8,128)S(1)}, f32[176,2,2048]{2,0,1:T(8,128)S(1)}) fusion(f32[176,2,2048]{2,1,0:T(2,128)S(1)} %copy-done, f32[176,1,2048]{2,0,1:T(8,128)} %bitcast.42, f32[176,1,2048]{2,0,1:T(8,128)} %bitcast.41, f32[176,2,2048]{2,1,0:T(2,128)} %param.12, f32[176,2,2048]{2,1,0:T(2,128)} %param.13), kind=kLoop, calls=%fused_computation.14 | loop fusion | flops 12255232 | bytes 20185088 | tf_op jit(solution)/shard_map/sub | solution.py:82
  455.9 3.8 copy.83
  459.7 3.8 copy.84
  463.5 3.8 copy.85
  (24 shorter events, 1.5 us)
Async XLA Ops:
  7.2 348.8 %reduce-scatter.7.cloned.1.call-start = ((), (), s32[]{:S(2)}) async-start(), calls=%async_computation.3 | async-start | bytes 12976128 | tf_op jit(solution)/shard_map/reduce_scatter | solution.py:68
  93.2 154.2 %slice-start = ((s8[4325376]{0:T(1024)(128)(4,1)}), s8[4194304]{0:T(1024)(128)(4,1)S(1)}, s32[]{:S(2)}) async-start(s8[4325376]{0:T(1024)(128)(4,1)} %bitcast.48), calls=%async_computation.5 | async-start | bytes 8388608
  237.7 9.7 %slice-start.1 = ((s8[4325376]{0:T(1024)(128)(4,1)}), s8[131072]{0:T(1024)(128)(4,1)S(1)}, s32[]{:S(2)}) async-start(s8[4325376]{0:T(1024)(128)(4,1)} %bitcast.48), calls=%async_computation.6 | async-start | bytes 262144
  269.2 177.5 %reduce-scatter.9.cloned.1.call-start = ((), (), s32[]{:S(2)}) async-start(), calls=%async_computation.4 | async-start | bytes 12976128 | tf_op jit(solution)/shard_map/reduce_scatter | solution.py:68
  294.6 152.1 %copy-start = (f32[176,2,2048]{2,1,0:T(2,128)S(1)}, f32[176,2,2048]{2,1,0:T(2,128)}, u32[]{:S(2)}) copy-start(f32[176,2,2048]{2,1,0:T(2,128)} %param.11) | copy-start | bytes 8650756
Sparse Core Ops, SparseCore 0:
  269.3 86.6 reduce-scatter.6
  359.5 87.1 reduce-scatter.8
where the time goes:
time: 475 us; the launch traced here: 474 us
  waiting for transfers between devices  152 us (32%)
  blocking collectives  144 us (30%)
  local copies, waits for them, and re-layouts  122 us (26%)
  matrix products  22.2 us (5%)
  other arithmetic  18.9 us (4%)
  between operations  14.2 us (3%)
    reduce_scatter x2, waiting for transfers between devices, shards(): lax.psum_scatter(one_term(jnp.int32(0), owned_rows * lax.axis_size('dp'))...  152 us
    all_to_all x1, blocking collectives, shards(): lax.all_to_all(scaled, 'expert', split_axis=1, concat_axis=1, tiled=True)  144 us
    unnamed x11, local copies, waits for them, and re-layouts  36.2 us
    scatter x1, local copies, waits for them, and re-layouts, slot_table(): slot_weight = jnp.zeros((window * capacity + 1,), route_weights.dtype).at...  23 us
    scatter x1, local copies, waits for them, and re-layouts, slot_table(): slot_anchor = jnp.zeros((window * capacity + 1,), jnp.int32).at[position....  23 us
    dot_general x2, matrix products, one_term(): jnp.einsum('rf,rd->fd', hidden_one, received_one, preferred_element_type=...  22.2 us
    gather x1, local copies, waits for them, and re-layouts, shards(): cotangent[slot_anchor].astype(jnp.float32) * slot_weight[:, None]  15.5 us
    convert_element_type x1, local copies, waits for them, and re-layouts, shards(): (cotangent[slot_anchor].astype(jnp.float32) * slot_weight[:, None]).astyp...  13 us
  transfers between devices with their start and end apart: 2, of which 2 were waited for; matrix products, arithmetic and copies ran while one was open for 5% of the time, Pallas kernels for 0%

commit v1 on v0

--- a/solution.py
+++ b/solution.py
@@ -53,7 +53,12 @@
         jnp.bfloat16
     )
     scaled = scaled.reshape(local_count, groups * capacity, width)
-    received = lax.all_to_all(scaled, "expert", split_axis=1, concat_axis=1, tiled=True)
+    received = jnp.concatenate(
+        lax.all_to_all(
+            jnp.stack(jnp.split(scaled, lax.axis_size("expert"), axis=1)), "expert", 0, 0
+        ),
+        axis=1,
+    )
     pieces = []
     for expert_local in range(local_count):
         hidden_one = hidden[expert_local]

time: 475 us -> 454 us (0.956)
  local copies, waits for them, and re-layouts: 122 us -> 102 us
    convert_element_type x1 -> x0, local copies, waits for them, and re-layouts: 13 us -> none  [shards(): (cotangent[slot_anchor].astype(jnp.float32) * slot_weight[:, None]).astyp...]
    slice x1, local copies, waits for them, and re-layouts: 9.74 us -> 1.11 us  [shards(): received_one = received[expert_local]]
where the time goes in v1:
time: 454 us; the launch traced here: 453 us
  waiting for transfers between devices  154 us (34%)
  blocking collectives  144 us (32%)
  local copies, waits for them, and re-layouts  102 us (22%)
  other arithmetic  19.7 us (4%)
  matrix products  18.2 us (4%)
  between operations  14.2 us (3%)
    reduce_scatter x2, waiting for transfers between devices, shards(): lax.psum_scatter(one_term(jnp.int32(0), owned_rows * lax.axis_size('dp'))...  154 us
    all_to_all x1, blocking collectives, shards(): lax.all_to_all(jnp.stack(jnp.split(scaled, lax.axis_size('expert'), axis=...  144 us
    unnamed x11, local copies, waits for them, and re-layouts  36.4 us
    scatter x1, local copies, waits for them, and re-layouts, slot_table(): slot_weight = jnp.zeros((window * capacity + 1,), route_weights.dtype).at...  23 us
    scatter x1, local copies, waits for them, and re-layouts, slot_table(): slot_anchor = jnp.zeros((window * capacity + 1,), jnp.int32).at[position....  23 us
    dot_general x2, matrix products, one_term(): jnp.einsum('rf,rd->fd', hidden_one, received_one, preferred_element_type=...  18.2 us
    gather x1, local copies, waits for them, and re-layouts, shards(): cotangent[slot_anchor].astype(jnp.float32) * slot_weight[:, None]  15.5 us
    sub x1, other arithmetic, shards(): new_master = master - learning_rate * update  9.23 us
  transfers between devices with their start and end apart: 2, of which 2 were waited for; matrix products, arithmetic and copies ran while one was open for 5% of the time, Pallas kernels for 0%

profile of v1, /device:TPU:0, one launch (start us, length us, event | category | flops | bytes accessed | tf_op | source)
XLA Modules:
  0.0 452.7 jit_solution(2854656655957121144)
XLA Ops:
  7.2 0.8 convert_reduce_fusion
  8.0 2.3 reduce-window.6
  10.8 0.8 select_reduce_fusion
  11.7 0.8 fusion.10
  12.5 0.8 broadcast_select_fusion
  14.0 0.4 reshape.76
  14.5 23.0 %scatter_custom_fusion.1 = f32[1537]{0:T(1024)S(1)} fusion(s32[6144]{0:T(1024)S(1)} %bitcast.55, f32[6144]{0:T(1024)S(1)} %reshape.101, f32[]{:T(128)} %constant.62.clone.1), kind=kCustom, calls=%fused_computation.49 | custom fusion | bytes 6152 | tf_op jit(solution)/shard_map/scatter | solution.py:37
  37.8 23.0 %scatter_custom_fusion = s32[1537]{0:T(1024)S(1)} fusion(s32[6144]{0:T(1024)S(1)} %bitcast.56, s32[6144]{0:T(1024)S(1)} %reshape.93, s32[]{:T(128)} %constant.29.clone.1), kind=kCustom, calls=%fused_computation.51 | custom fusion | bytes 6152 | tf_op jit(solution)/shard_map/scatter | solution.py:31
  60.9 15.5 %gather_fusion = bf16[1536,2048]{1,0:T(8,128)(2,1)} fusion(bf16[1024,2048]{1,0:T(8,128)(2,1)} %param.7, s32[2048]{0:T(1024)S(1)} %pad_clamp_fusion), kind=kCustom, calls=%fused_computation | custom fusion | bytes 12589056 | tf_op jit(solution)/shard_map/gather | solution.py:52
  76.3 3.9 fusion
  80.2 1.1 slice_bitcast_fusion.3
  81.3 0.8 pad_maximum_fusion
  82.2 144.5 %all_to_all.5 = bf16[4,2,192,2048]{3,2,1,0:T(8,128)(2,1)S(1)} all-to-all(bf16[4,2,192,2048]{3,2,1,0:T(8,128)(2,1)S(1)} %pad_maximum_fusion), channel_id=1, replica_groups=mesh['dp'=8,'expert'=4] {'expert'}, dimensions={0} | all-to-all | bytes 12582912 | tf_op jit(solution)/shard_map/all_to_all | solution.py:57
  226.7 1.1 fusion.23
  227.8 7.8 %convolution_bitcast_fusion = f32[1408,2048]{0,1:T(8,128)} fusion(bf16[768,2048]{1,0:T(8,128)(2,1)S(1)} %bitcast.50, bf16[2,768,1408]{2,1,0:T(8,128)(2,1)S(1)} %bitcast.59), kind=kOutput, calls=%fused_computation.5 | convolution fusion | flops 4429185024 | bytes 16842752 | tf_op jit(solution)/shard_map/rf,rd->fd/dot_general | solution.py:68
  235.7 12.0 %copy.65 = f32[1408,2048]{1,0:T(8,128)} copy(f32[1408,2048]{0,1:T(8,128)} %convolution_bitcast_fusion) | data formatting | bytes 23068672
  247.8 10.4 %convolution_bitcast_fusion.1 = f32[1408,2048]{0,1:T(8,128)} fusion(bf16[768,2048]{1,0:T(8,128)(2,1)S(1)} %bitcast.49, bf16[2,768,1408]{2,1,0:T(8,128)(2,1)} %param.10), kind=kOutput, calls=%fused_computation.6 | convolution fusion | flops 4429185024 | bytes 16842752 | tf_op jit(solution)/shard_map/rf,rd->fd/dot_general | solution.py:68
  258.1 13.0 %copy.63 = f32[1408,2048]{1,0:T(8,128)} copy(f32[1408,2048]{0,1:T(8,128)} %convolution_bitcast_fusion.1) | data formatting | bytes 23068672
  271.1 63.4 %reduce-scatter.9.cloned.1.call-done = f32[176,2048]{1,0:T(8,128)} async-done(((f32[1408,2048]{1,0:T(8,128)}), f32[176,2048]{1,0:T(8,128)}) %reduce-scatter.9.cloned.1.call-update) | async-done | bytes 1441808 | tf_op jit(solution)/shard_map/reduce_scatter | solution.py:73
  334.5 90.7 %reduce-scatter.7.cloned.1.call-done = f32[176,2048]{1,0:T(8,128)} async-done(((f32[1408,2048]{1,0:T(8,128)}), f32[176,2048]{1,0:T(8,128)}) %reduce-scatter.7.cloned.1.call-update) | async-done | bytes 1441808 | tf_op jit(solution)/shard_map/reduce_scatter | solution.py:73
  425.2 9.2 %multiply_subtract_fusion = (f32[176,2,2048]{2,0,1:T(8,128)S(1)}, f32[176,2,2048]{2,0,1:T(8,128)S(1)}, f32[176,2,2048]{2,0,1:T(8,128)S(1)}) fusion(f32[176,2,2048]{2,1,0:T(2,128)S(1)} %copy-done, f32[176,1,2048]{2,0,1:T(8,128)} %bitcast.51, f32[176,1,2048]{2,0,1:T(8,128)} %bitcast.52, f32[176,2,2048]{2,1,0:T(2,128)} %param.12, f32[176,2,2048]{2,1,0:T(2,128)} %param.13), kind=kLoop, calls=%fused_computation.13 | loop fusion | flops 12255232 | bytes 20185088 | tf_op jit(solution)/shard_map/sub | solution.py:87
  434.4 3.8 copy.60
  438.2 3.8 copy.61
  442.1 3.8 copy.62
  (25 shorter events, 1.9 us)
Async XLA Ops:
  7.2 327.4 %reduce-scatter.9.cloned.1.call-start = ((), (), s32[]{:S(2)}) async-start(), calls=%async_computation.4 | async-start | bytes 12976128 | tf_op jit(solution)/shard_map/reduce_scatter | solution.py:73
  82.2 145.6 %slice-start = ((s8[4325376]{0:T(1024)(128)(4,1)}), s8[4194304]{0:T(1024)(128)(4,1)S(1)}, s32[]{:S(2)}) async-start(s8[4325376]{0:T(1024)(128)(4,1)} %bitcast.58), calls=%async_computation.5 | async-start | bytes 8388608
  226.7 1.1 slice-start.1
  247.7 177.5 %reduce-scatter.7.cloned.1.call-start = ((), (), s32[]{:S(2)}) async-start(), calls=%async_computation.3 | async-start | bytes 12976128 | tf_op jit(solution)/shard_map/reduce_scatter | solution.py:73
  271.1 154.1 %copy-start = (f32[176,2,2048]{2,1,0:T(2,128)S(1)}, f32[176,2,2048]{2,1,0:T(2,128)}, u32[]{:S(2)}) copy-start(f32[176,2,2048]{2,1,0:T(2,128)} %param.11) | copy-start | bytes 8650756
Sparse Core Ops, SparseCore 0:
  247.8 86.6 reduce-scatter.8
  338.0 87.1 reduce-scatter.6
